TPU v7x, 512 devices: a whole 4x4x16 slice. The times are simulated.
512 devices in a mesh: tm: 16 (over z_lo, core), inp: 32 (over x, y, z_hi).
Axes of the slice: x: 4, y: 4, z: 16 (z_hi: 2, z_lo: 8; z = z_hi * 8 + z_lo), core: 2. Of those that a mesh axis runs over, the one named last changes fastest.
Arguments:
- voltage: int32 [256, 2097152], P('inp', 'tm'), may hold values from -127 to 127
- taps: float32 [4, 512], replicated, may hold values from -0.0625 to 0.0625
- chan_table: int32 [256], replicated, may hold values from 0 to 255, each once
Outputs:
- visibility: float32 [256, 128, 256], P('tm', 'inp')
- beam: float32 [128, 4096], P('inp', 'tm')
Inputs may be any that keep to these rules, and one draw needn't show every extreme that they name: `chan_table`: each channel number appears once.
All inputs are finite; a program needn't handle non-finite values.
Results may differ from a plain program's by a relative error of at most 0.0016.
Values may be sent and summed in bfloat16 or wider, within the bound.
A program may use at most 64 MiB of HBM per device.

v0:
```python
import math

import jax
import jax.numpy as jnp
from jax import lax
from jax.sharding import PartitionSpec as P

NIN = 256
P_SIZE = 512
TAPS = 4
NCH = 128


def passed_along(block, axis, distance):
    devices = range(lax.axis_size(axis))
    route = [(i - distance, i) for i in devices if i - distance in devices]
    return lax.ppermute(block, axis, route)


def dft_table(chan_table):
    chosen = chan_table[:NCH]
    points = jnp.arange(P_SIZE, dtype=jnp.int32)
    phase = chosen[:, None] * points[None, :] % P_SIZE
    angle = phase.astype(jnp.float32) * (2.0 * math.pi / P_SIZE)
    factor = 1.0 / math.sqrt(P_SIZE)
    table = jnp.stack([jnp.cos(angle) * factor, -jnp.sin(angle) * factor], axis=1)
    return table.astype(jnp.bfloat16)


def split_parts(received):
    parts = received[0]
    combined = jnp.concatenate([parts[:, 0], parts[:, 1]], axis=-1)
    rotated = jnp.concatenate([parts[:, 1], -parts[:, 0]], axis=-1)
    return (combined, rotated)


def packed_rows(combined, rotated, count):
    real_part = jnp.einsum("cas,cbs->acb", combined, combined, preferred_element_type=jnp.float32)
    imag_part = jnp.einsum("cas,cbs->acb", rotated, combined, preferred_element_type=jnp.float32)
    row_index = jnp.arange(count, dtype=jnp.int32)
    col_index = jnp.arange(combined.shape[1], dtype=jnp.int32)
    upper = (row_index[:, None] <= col_index[None, :])[:, None, :]
    return jnp.where(upper, real_part, imag_part)


def on_device(voltage, taps, chan_table):
    inputs_here = voltage.shape[0]
    spectra_here = voltage.shape[1] // P_SIZE
    groups = lax.axis_size("inp")
    volts = voltage.astype(jnp.bfloat16)
    tail = volts[:, (spectra_here - TAPS + 1) * P_SIZE :]
    earlier = passed_along(tail, "tm", 1)
    extended = jnp.concatenate([earlier, volts], axis=1).reshape(
        inputs_here, spectra_here + TAPS - 1, P_SIZE
    )
    filtered = jnp.zeros((inputs_here, spectra_here, P_SIZE), jnp.float32)
    for tap_index in range(TAPS):
        filtered = filtered + taps[tap_index] * extended[
            :, tap_index : tap_index + spectra_here, :
        ].astype(jnp.float32)
    filtered = filtered.astype(jnp.bfloat16)
    table = dft_table(chan_table).reshape(groups, NCH // groups, 2, P_SIZE)
    spectra = jnp.einsum(
        "gcqp,isp->gcqis", table, filtered, preferred_element_type=jnp.float32
    ).astype(jnp.bfloat16)
    total = spectra_here * lax.axis_size("tm")
    power = jnp.sum(jnp.square(spectra.astype(jnp.float32)), axis=(2, 3)).reshape(NCH, spectra_here)
    beam = lax.psum_scatter(power, "inp", scatter_dimension=0, tiled=True) / NIN
    received = lax.all_to_all(spectra, "inp", split_axis=0, concat_axis=3, tiled=True)
    combined, rotated = split_parts(received)
    packed = packed_rows(combined, rotated, combined.shape[1])
    visibility = lax.psum_scatter(packed, "tm", scatter_dimension=0, tiled=True)
    return (visibility / total, beam)


def solution(mesh):
    in_specs = (P("inp", "tm"), P(), P())
    out_specs = (P("tm", "inp", None), P("inp", "tm"))
    return jax.shard_map(
        on_device, mesh=mesh, in_specs=in_specs, out_specs=out_specs, check_vma=False
    )
```

profile of v0, /device:TPU:1, one launch (start us, length us, event | category | flops | bytes accessed | tf_op | source)
XLA Modules:
  0.0 836.1 jit_solution(16190021593114257303)
XLA Ops:
  7.2 0.0 slice-start
  7.2 0.0 copy-start
  7.2 2.4 convert_element_type.43
  9.6 4.9 collective-permute-start
  14.5 0.0 slice-done
  14.5 0.1 mul.109
  14.6 0.1 copy.30
  14.7 1.2 multiply_convert_fusion.1
  16.0 0.0 copy-done
  16.0 2.4 collective-permute-done
  18.4 0.2 pad_maximum_fusion
  18.6 0.9 fusion.22
  19.5 5.9 multiply_reduce_fusion
  25.4 1.6 copy.35
  26.9 17.0 %all-to-all-start = ((bf16[32,4,2,8,256]{4,3,2,1,0:T(8,128)(2,1)}), bf16[32,4,2,8,256]{4,3,2,1,0:T(8,128)(2,1)S(1)}, u32[]{:S(2)}, u32[]{:S(2)}) async-start(bf16[32,4,2,8,256]{4,3,2,1,0:T(8,128)(2,1)} %copy.35), calls=%async_computation | async-start | bytes 2097152 | tf_op jit(solution)/shard_map/all_to_all | solution.py:69
  44.0 0.0 all-reduce.7.cloned.1.call-start
  44.1 0.1 copy.40
  44.2 0.7 reshape.126
  44.9 0.0 all-reduce.7.cloned.1.call-update
  44.9 0.0 all-reduce.5.cloned.1.call-start
  44.9 31.1 %all-to-all-done = bf16[32,4,2,8,256]{4,3,2,1,0:T(8,128)(2,1)S(1)} async-done(((bf16[32,4,2,8,256]{4,3,2,1,0:T(8,128)(2,1)}), bf16[32,4,2,8,256]{4,3,2,1,0:T(8,128)(2,1)S(1)}, u32[]{:S(2)}, u32[]{:S(2)}) %all-to-all-start) | async-done | bytes 1048608 | tf_op jit(solution)/shard_map/all_to_all | solution.py:69
  76.0 0.1 copy.74
  76.1 0.1 slice_bitcast_fusion.1
  76.2 0.5 convolution_bitcast_fusion
  76.7 0.5 fusion.6
  77.1 1.4 copy.39
  78.5 0.0 all-reduce.5.cloned.1.call-update
  78.5 1.3 dynamic-slice
  79.8 1.3 dynamic-slice.2
  82.4 526.8 %all-reduce.7.cloned.1.call-done = f32[128,256]{1,0:T(8,128)} async-done(((f32[128,256]{1,0:T(8,128)}), f32[128,256]{1,0:T(8,128)}) %all-reduce.7.cloned.1.call-update) | async-done | bytes 131088
  609.2 1.3 dynamic-slice_multiply_fusion.1
  610.4 217.4 %all-reduce.5.cloned.1.call-done = f32[256,4,256]{2,1,0:T(4,128)} async-done(((f32[256,4,256]{2,1,0:T(4,128)}), f32[256,4,256]{2,1,0:T(4,128)}) %all-reduce.5.cloned.1.call-update) | async-done | bytes 1048592
  827.8 1.5 dynamic-slice_multiply_fusion
  (4 shorter events, 0.1 us)
Async XLA Ops:
  7.2 7.4 slice-start
  7.2 8.8 %copy-start = (f32[4,512]{1,0:T(4,128)S(1)}, f32[4,512]{1,0:T(4,128)}, u32[]{:S(2)}) copy-start(f32[4,512]{1,0:T(4,128)} %param.4) | copy-start | bytes 24580
  9.6 8.8 %collective-permute-start = (bf16[8,1536]{1,0:T(8,128)(2,1)S(1)}, bf16[8,1536]{1,0:T(8,128)(2,1)S(1)}, u32[]{:S(2)}, u32[]{:S(2)}) collective-permute-start(bf16[8,1536]{1,0:T(8,128)(2,1)S(1)} %slice.54), channel_id=1, source_target_pairs={{0,32},{32,64},{64,96},{96,128},{128,160},{160,192},{192,224},{224... | collective-permute-start | bytes 73736 | tf_op jit(solution)/shard_map/ppermute | solution.py:17
  26.9 49.0 %all-to-all-start = ((bf16[32,4,2,8,256]{4,3,2,1,0:T(8,128)(2,1)}), bf16[32,4,2,8,256]{4,3,2,1,0:T(8,128)(2,1)S(1)}, u32[]{:S(2)}, u32[]{:S(2)}) async-start(bf16[32,4,2,8,256]{4,3,2,1,0:T(8,128)(2,1)} %copy.35), calls=%async_computation | async-start | bytes 2097152 | tf_op jit(solution)/shard_map/all_to_all | solution.py:69
  44.0 565.2 %all-reduce.7.cloned.1.call-start = ((), (), s32[]{:S(2)}) async-start(), calls=%async_computation.2 | async-start | bytes 262144
  44.9 782.9 %all-reduce.5.cloned.1.call-start = ((), (), s32[]{:S(2)}) async-start(), calls=%async_computation.1 | async-start | bytes 2097152
Sparse Core Ops, SparseCore 0:
  47.7 561.4 all-reduce.6
  612.1 215.6 all-reduce.4
where the time goes:
time: 837 us; the launch traced here: 836 us
  waiting for transfers between devices  778 us (93%)
  starting transfers between devices  22 us (3%)
  between operations  15.5 us (2%)
    unnamed x4, waiting for transfers between devices  744 us
    all_to_all x1, waiting for transfers between devices, on_device(): lax.all_to_all(spectra, 'inp', split_axis=0, concat_axis=3, tiled=True)  31.1 us
    all_to_all x1, starting transfers between devices, on_device(): lax.all_to_all(spectra, 'inp', split_axis=0, concat_axis=3, tiled=True)  17 us
  transfers between devices with their start and end apart: 4, of which 4 were waited for; matrix products, arithmetic and copies ran while one was open for 1% of the time, Pallas kernels for 0%

commit v1 on v0

v1 whole, which is shorter than its diff:
```python
import math

import jax
import jax.numpy as jnp
from jax import lax
from jax.sharding import Mesh, PartitionSpec as P

NIN = 256
P_SIZE = 512
TAPS = 4
NCH = 128
ZG, ZQ, CORE, INP = 2, 4, 2, 32
TM = ("zg", "zq", "core")


def dft_table(chan_table):
    chosen = chan_table[:NCH]
    points = jnp.arange(P_SIZE, dtype=jnp.int32)
    phase = chosen[:, None] * points[None, :] % P_SIZE
    angle = phase.astype(jnp.float32) * (2.0 * math.pi / P_SIZE)
    factor = 1.0 / math.sqrt(P_SIZE)
    table = jnp.stack([jnp.cos(angle) * factor, -jnp.sin(angle) * factor], axis=1)
    return table.astype(jnp.bfloat16)


def on_device(voltage, taps, chan_table):
    inputs_here = voltage.shape[0]
    spectra_here = voltage.shape[1] // P_SIZE
    blocks = ZG * ZQ * CORE
    volts = voltage.astype(jnp.bfloat16)
    tail = volts[:, (spectra_here - TAPS + 1) * P_SIZE :]
    earlier = lax.ppermute(tail, TM, [(i - 1, i) for i in range(1, blocks)])
    extended = jnp.concatenate([earlier, volts], axis=1).reshape(
        inputs_here, spectra_here + TAPS - 1, P_SIZE
    )
    filtered = jnp.zeros((inputs_here, spectra_here, P_SIZE), jnp.float32)
    for tap_index in range(TAPS):
        filtered = filtered + taps[tap_index] * extended[
            :, tap_index : tap_index + spectra_here, :
        ].astype(jnp.float32)
    filtered = filtered.astype(jnp.bfloat16)
    table = dft_table(chan_table).reshape(INP, ZQ, 2, P_SIZE).transpose(1, 0, 2, 3)
    table = table.reshape(ZQ * INP, 2, P_SIZE)
    spectra = jnp.einsum(
        "cqp,isp->cqis", table, filtered, preferred_element_type=jnp.float32
    ).astype(jnp.bfloat16)
    received = lax.all_to_all(spectra, ("zq", "inp"), split_axis=0, concat_axis=0, tiled=True)
    received = received.reshape(ZQ, INP, 2, inputs_here, spectra_here)
    parts = received.transpose(2, 0, 1, 3, 4).reshape(2, ZQ, NIN, spectra_here)
    power = jnp.sum(jnp.square(parts.astype(jnp.float32)), axis=(0, 2)) / NIN
    here = lax.axis_index("zq")
    beam_parts = [lax.dynamic_index_in_dim(power, here, 0, keepdims=False)]
    for step in range(1, ZQ):
        mine = lax.dynamic_index_in_dim(power, (here + step) % ZQ, 0, keepdims=False)
        beam_parts.append(
            lax.ppermute(mine, "zq", [(i, (i + step) % ZQ) for i in range(ZQ)])
        )
    stacked = jnp.stack(beam_parts)
    order = (here - jnp.arange(ZQ, dtype=jnp.int32)) % ZQ
    select = (order[:, None] == jnp.arange(ZQ, dtype=jnp.int32)[None, :]).astype(jnp.float32)
    beam = jnp.sum(jnp.where(select[:, :, None] > 0, stacked[:, None, :], 0.0), axis=0)
    re_part = jnp.einsum("qzas,qzbs->ab", parts, parts, preferred_element_type=jnp.float32)
    cross = jnp.einsum("zas,zbs->ab", parts[1], parts[0], preferred_element_type=jnp.float32)
    index = jnp.arange(NIN, dtype=jnp.int32)
    upper = index[:, None] <= index[None, :]
    packed = jnp.where(upper, re_part, cross - cross.T)
    packed = packed.reshape(ZG * ZQ, CORE, NIN // blocks, NIN)
    core = lax.axis_index("core")
    keep = jnp.where(core == 0, packed[:, 0], packed[:, 1])
    give = jnp.where(core == 0, packed[:, 1], packed[:, 0])
    pair = keep + lax.ppermute(give, "core", [(0, 1), (1, 0)])
    sums = lax.all_to_all(pair, ("zg", "zq"), split_axis=0, concat_axis=0, tiled=True)
    sums = sums.reshape(ZG, ZQ, NIN // blocks, NIN)
    visibility = (sums[0] + sums[1]).transpose(1, 0, 2)
    total = spectra_here * blocks
    return (visibility / total, beam)


def solution(mesh):
    fine = Mesh(mesh.devices.reshape(ZG, ZQ, CORE, INP), TM + ("inp",))
    in_specs = (P("inp", TM), P(), P())
    out_specs = (P(TM, "inp", None), P("inp", TM))
    return jax.shard_map(
        on_device, mesh=fine, in_specs=in_specs, out_specs=out_specs, check_vma=False
    )
```

time: 837 us -> 119 us (0.14)
  waiting for transfers between devices: 778 us -> 60.3 us
  starting transfers between devices: 22 us -> 41.6 us
  between operations: 15.5 us -> 0.89 us
    unnamed x4 -> x0, waiting for transfers between devices: 744 us -> none
    all_to_all x1 -> x2, waiting for transfers between devices: 31.1 us -> 55.5 us  [the longest x1 55.5 us: on_device(): lax.all_to_all(spectra, ('zq', 'inp'), split_axis=0, concat_axis=0, tiled...]
    ppermute x1 -> x5, starting transfers between devices: 4.92 us -> 18.3 us  [the longest x3 10.5 us: on_device(): lax.ppermute(mine, 'zq', [(i, (i + step) % ZQ) for i in range(ZQ)])]
    all_to_all x1 -> x2, starting transfers between devices: 17 us -> 23.4 us  [the longest x1 18.9 us: on_device(): lax.all_to_all(spectra, ('zq', 'inp'), split_axis=0, concat_axis=0, tiled...]
  transfers between devices with their start and end apart: 4 -> 7, of which waited for: 4 -> 4; matrix products, arithmetic and copies ran while one was open for 1% -> 2% of each run, Pallas kernels for 0% -> 0%
where the time goes in v1:
time: 119 us; the launch traced here: 118 us
  waiting for transfers between devices  60.3 us (51%)
  starting transfers between devices  41.6 us (35%)
  matrix products  6.64 us (6%)
  other arithmetic  5.59 us (5%)
  local copies, waits for them, and re-layouts  3.47 us (3%)
    all_to_all x1, waiting for transfers between devices, on_device(): lax.all_to_all(spectra, ('zq', 'inp'), split_axis=0, concat_axis=0, tiled...  55.5 us
    all_to_all x1, starting transfers between devices, on_device(): lax.all_to_all(spectra, ('zq', 'inp'), split_axis=0, concat_axis=0, tiled...  18.9 us
    ppermute x3, starting transfers between devices, on_device(): lax.ppermute(mine, 'zq', [(i, (i + step) % ZQ) for i in range(ZQ)])  10.5 us
    dot_general x1, matrix products, on_device(): jnp.einsum('cqp,isp->cqis', table, filtered, preferred_element_type=jnp.f...  5.82 us
    ppermute x1, starting transfers between devices, on_device(): earlier = lax.ppermute(tail, TM, [(i - 1, i) for i in range(1, blocks)])  4.92 us
    all_to_all x1, starting transfers between devices, on_device(): lax.all_to_all(pair, ('zg', 'zq'), split_axis=0, concat_axis=0, tiled=True)  4.47 us
    ppermute x1, starting transfers between devices, on_device(): pair = keep + lax.ppermute(give, 'core', [(0, 1), (1, 0)])  2.88 us
    convert_element_type x1, other arithmetic, on_device(): volts = voltage.astype(jnp.bfloat16)  2.4 us
  transfers between devices with their start and end apart: 7, of which 4 were waited for; matrix products, arithmetic and copies ran while one was open for 2% of the time, Pallas kernels for 0%

profile of v1, /device:TPU:1, one launch (start us, length us, event | category | flops | bytes accessed | tf_op | source)
XLA Modules:
  0.0 118.5 jit_solution(1992621437541462051)
XLA Ops:
  0.6 0.0 copy-start
  0.6 0.0 slice-start
  0.7 2.4 %convert_element_type.51 = bf16[8,131072]{1,0:T(8,128)(2,1)S(1)} convert(s32[8,131072]{1,0:T(8,128)} %param.3) | non-fusion elementwise | flops 1048576 | bytes 6291456 | tf_op jit(solution)/shard_map/convert_element_type | solution.py:30
  3.1 4.9 %collective-permute-start = (bf16[8,1536]{1,0:T(8,128)(2,1)S(1)}, bf16[8,1536]{1,0:T(8,128)(2,1)S(1)}, u32[]{:S(2)}, u32[]{:S(2)}) collective-permute-start(bf16[8,1536]{1,0:T(8,128)(2,1)S(1)} %slice.74), channel_id=1, source_target_pairs={{0,32},{32,64},{64,96},{96,128},{128,160},{160,192},{192,224},{224... | collective-permute-start | bytes 73736 | tf_op jit(solution)/shard_map/ppermute | solution.py:32
  8.0 0.0 copy-done
  8.0 0.0 slice-done
  8.0 0.1 mul.109
  8.1 0.1 copy.38
  8.2 1.2 %multiply_convert_fusion.1 = (bf16[32,4,1,512]{3,0,1,2:T(8,128)(2,1)S(1)}, bf16[32,4,1,512]{3,0,1,2:T(8,128)(2,1)S(1)}) fusion(s32[32,4]{0,1:T(4,128)S(1)} %copy.38), kind=kLoop, calls=%fused_computation.23 | loop fusion | flops 1245184 | bytes 262656 | tf_op jit(solution)/shard_map/convert
  9.5 2.4 %collective-permute-done = bf16[8,1536]{1,0:T(8,128)(2,1)S(1)} collective-permute-done((bf16[8,1536]{1,0:T(8,128)(2,1)S(1)}, bf16[8,1536]{1,0:T(8,128)(2,1)S(1)}, u32[]{:S(2)}, u32[]{:S(2)}) %collective-permute-start) | collective-permute-done | bytes 24608 | tf_op jit(solution)/shard_map/ppermute | solution.py:32
  11.9 0.2 pad_maximum_fusion
  12.1 0.8 fusion.18
  12.9 5.8 %fusion.3 = bf16[128,2,8,256]{3,0,2,1:T(8,128)(2,1)S(1)} fusion(bf16[128,2,512,1]{2,0,3,1:T(8,128)(2,1)S(1)} %bitcast.77, bf16[8,256,512]{2,0,1:T(8,128)(2,1)S(1)} %get-tuple-element.9, bf16[8,256,512]{2,0,1:T(8,128)(2,1)S(1)} %get-tuple-element.7, bf16[8,256,512]{2,0,1:T(8,128)(2,1)S(1)} %get-tuple-element.8, ...), kind=kOutput, calls=%fused_computation.5 | convolution fusion | flops 549978112 | bytes 9707520 | tf_op jit(solution)/shard_map/cqp,isp->cqis/dot_general | solution.py:44
  18.8 1.6 %copy.43 = bf16[128,2,8,256]{3,2,1,0:T(8,128)(2,1)} copy(bf16[128,2,8,256]{3,0,2,1:T(8,128)(2,1)S(1)} %fusion.3) | data formatting | bytes 2097152 | tf_op jit(solution)/shard_map/convert_element_type | solution.py:46
  20.3 18.9 %all-to-all-start = ((bf16[128,2,8,256]{3,2,1,0:T(8,128)(2,1)}), bf16[128,2,8,256]{3,2,1,0:T(8,128)(2,1)S(1)}, u32[]{:S(2)}, u32[]{:S(2)}) async-start(bf16[128,2,8,256]{3,2,1,0:T(8,128)(2,1)} %copy.43), calls=%async_computation | async-start | bytes 2097152 | tf_op jit(solution)/shard_map/all_to_all | solution.py:47
  39.3 55.5 %all-to-all-done = bf16[128,2,8,256]{3,2,1,0:T(8,128)(2,1)S(1)} async-done(((bf16[128,2,8,256]{3,2,1,0:T(8,128)(2,1)}), bf16[128,2,8,256]{3,2,1,0:T(8,128)(2,1)S(1)}, u32[]{:S(2)}, u32[]{:S(2)}) %all-to-all-start) | async-done | bytes 1048608 | tf_op jit(solution)/shard_map/all_to_all | solution.py:47
  94.8 0.2 multiply_reduce_fusion
  95.0 0.1 copy_bitcast_fusion
  95.1 0.3 convolution_bitcast_fusion
  95.4 0.1 copy.45
  95.6 0.5 fusion.6
  96.1 2.9 %collective-permute-start.1 = (f32[8,16,256]{2,1,0:T(8,128)S(1)}, f32[8,16,256]{2,1,0:T(8,128)S(1)}, u32[]{:S(2)}, u32[]{:S(2)}) collective-permute-start(f32[8,16,256]{2,1,0:T(8,128)S(1)} %select_bitcast_fusion), channel_id=1, source_target_pairs={{0,32},{32,0},{1,33},{33,1},{2,34},{34,2},{3,35},{35,3},{4,36},{36... | collective-permute-start | bytes 393224 | tf_op jit(solution)/shard_map/ppermute | solution.py:71
  99.0 1.0 collective-permute-done.1
  99.9 0.7 bitcast_add_fusion
  100.6 4.5 %all-to-all-start.1 = ((f32[8,16,256]{2,1,0:T(8,128)}), f32[8,16,256]{2,1,0:T(8,128)S(1)}, u32[]{:S(2)}, u32[]{:S(2)}) async-start(f32[8,16,256]{2,1,0:T(8,128)} %bitcast_add_fusion), calls=%async_computation.1 | async-start | bytes 262144 | tf_op jit(solution)/shard_map/all_to_all | solution.py:72
  105.1 3.9 %collective-permute-start.2 = (f32[256]{0:T(256)S(1)}, f32[256]{0:T(256)S(1)}, u32[]{:S(2)}, u32[]{:S(2)}) collective-permute-start(f32[256]{0:T(256)S(1)} %bitcast.84), channel_id=1, source_target_pairs={{0,64},{64,128},{128,192},{192,0},{1,65},{65,129},{129,193},{193,1... | collective-permute-start | bytes 3080 | tf_op jit(solution)/shard_map/ppermute | solution.py:56
  109.0 3.5 %collective-permute-start.3 = (f32[256]{0:T(256)S(1)}, f32[256]{0:T(256)S(1)}, u32[]{:S(2)}, u32[]{:S(2)}) collective-permute-start(f32[256]{0:T(256)S(1)} %bitcast.83), channel_id=1, source_target_pairs={{0,128},{64,192},{128,0},{192,64},{1,129},{65,193},{129,1},{193,65... | collective-permute-start | bytes 3080 | tf_op jit(solution)/shard_map/ppermute | solution.py:56
  112.5 3.1 %collective-permute-start.4 = (f32[256]{0:T(256)S(1)}, f32[256]{0:T(256)S(1)}, u32[]{:S(2)}, u32[]{:S(2)}) collective-permute-start(f32[256]{0:T(256)S(1)} %bitcast.82), channel_id=1, source_target_pairs={{0,192},{64,0},{128,64},{192,128},{1,193},{65,1},{129,65},{193,129... | collective-permute-start | bytes 3080 | tf_op jit(solution)/shard_map/ppermute | solution.py:56
  115.6 0.1 convert_compare_fusion
  115.6 0.0 collective-permute-done.2
  115.6 0.0 collective-permute-done.3
  115.7 1.4 %collective-permute-done.4 = f32[256]{0:T(256)S(1)} collective-permute-done((f32[256]{0:T(256)S(1)}, f32[256]{0:T(256)S(1)}, u32[]{:S(2)}, u32[]{:S(2)}) %collective-permute-start.4) | collective-permute-done | bytes 1056 | tf_op jit(solution)/shard_map/ppermute | solution.py:56
  117.1 0.7 select_reduce_fusion
  117.8 0.0 all-to-all-done.1
  117.8 0.7 copy.48
  (9 shorter events, 0.1 us)
Async XLA Ops:
  0.6 7.4 %copy-start = (f32[4,512]{1,0:T(4,128)S(1)}, f32[4,512]{1,0:T(4,128)}, u32[]{:S(2)}) copy-start(f32[4,512]{1,0:T(4,128)} %param.4) | copy-start | bytes 24580
  0.6 7.4 %slice-start = ((s32[256]{0:T(256)}), s32[128]{0:T(128)S(1)}, s32[]{:S(2)}) async-start(s32[256]{0:T(256)} %param.5), calls=%async_computation.2 | async-start | bytes 1024 | tf_op jit(solution)/shard_map/slice | solution.py:17
  3.1 8.8 %collective-permute-start = (bf16[8,1536]{1,0:T(8,128)(2,1)S(1)}, bf16[8,1536]{1,0:T(8,128)(2,1)S(1)}, u32[]{:S(2)}, u32[]{:S(2)}) collective-permute-start(bf16[8,1536]{1,0:T(8,128)(2,1)S(1)} %slice.74), channel_id=1, source_target_pairs={{0,32},{32,64},{64,96},{96,128},{128,160},{160,192},{192,224},{224... | collective-permute-start | bytes 73736 | tf_op jit(solution)/shard_map/ppermute | solution.py:32
  20.3 74.5 %all-to-all-start = ((bf16[128,2,8,256]{3,2,1,0:T(8,128)(2,1)}), bf16[128,2,8,256]{3,2,1,0:T(8,128)(2,1)S(1)}, u32[]{:S(2)}, u32[]{:S(2)}) async-start(bf16[128,2,8,256]{3,2,1,0:T(8,128)(2,1)} %copy.43), calls=%async_computation | async-start | bytes 2097152 | tf_op jit(solution)/shard_map/all_to_all | solution.py:47
  96.1 3.9 %collective-permute-start.1 = (f32[8,16,256]{2,1,0:T(8,128)S(1)}, f32[8,16,256]{2,1,0:T(8,128)S(1)}, u32[]{:S(2)}, u32[]{:S(2)}) collective-permute-start(f32[8,16,256]{2,1,0:T(8,128)S(1)} %select_bitcast_fusion), channel_id=1, source_target_pairs={{0,32},{32,0},{1,33},{33,1},{2,34},{34,2},{3,35},{35,3},{4,36},{36... | collective-permute-start | bytes 393224 | tf_op jit(solution)/shard_map/ppermute | solution.py:71
  100.6 17.2 %all-to-all-start.1 = ((f32[8,16,256]{2,1,0:T(8,128)}), f32[8,16,256]{2,1,0:T(8,128)S(1)}, u32[]{:S(2)}, u32[]{:S(2)}) async-start(f32[8,16,256]{2,1,0:T(8,128)} %bitcast_add_fusion), calls=%async_computation.1 | async-start | bytes 262144 | tf_op jit(solution)/shard_map/all_to_all | solution.py:72
  105.1 10.6 %collective-permute-start.2 = (f32[256]{0:T(256)S(1)}, f32[256]{0:T(256)S(1)}, u32[]{:S(2)}, u32[]{:S(2)}) collective-permute-start(f32[256]{0:T(256)S(1)} %bitcast.84), channel_id=1, source_target_pairs={{0,64},{64,128},{128,192},{192,0},{1,65},{65,129},{129,193},{193,1... | collective-permute-start | bytes 3080 | tf_op jit(solution)/shard_map/ppermute | solution.py:56
  109.0 6.7 %collective-permute-start.3 = (f32[256]{0:T(256)S(1)}, f32[256]{0:T(256)S(1)}, u32[]{:S(2)}, u32[]{:S(2)}) collective-permute-start(f32[256]{0:T(256)S(1)} %bitcast.83), channel_id=1, source_target_pairs={{0,128},{64,192},{128,0},{192,64},{1,129},{65,193},{129,1},{193,65... | collective-permute-start | bytes 3080 | tf_op jit(solution)/shard_map/ppermute | solution.py:56
  112.5 4.6 %collective-permute-start.4 = (f32[256]{0:T(256)S(1)}, f32[256]{0:T(256)S(1)}, u32[]{:S(2)}, u32[]{:S(2)}) collective-permute-start(f32[256]{0:T(256)S(1)} %bitcast.82), channel_id=1, source_target_pairs={{0,192},{64,0},{128,64},{192,128},{1,193},{65,1},{129,65},{193,129... | collective-permute-start | bytes 3080 | tf_op jit(solution)/shard_map/ppermute | solution.py:56

commit v2 on v0

v2 whole, which is shorter than its diff:
```python
import math

import jax
import jax.numpy as jnp
from jax import lax
from jax.experimental import pallas as pl
from jax.experimental.pallas import tpu as pltpu
from jax.sharding import PartitionSpec as P

NIN = 256
P_SIZE = 512
TAPS = 4
NCH = 128
ZLO, ZQ, INP = 8, 4, 32
TM = 2 * ZLO
GROUP = ZQ * INP
MESH = pl.DeviceIdType.MESH
CHUNKS = 4


def dft_table(chan_table):
    chosen = chan_table[:NCH].reshape(INP, ZQ).T.reshape(NCH)
    points = jnp.arange(P_SIZE, dtype=jnp.int32)
    phase = chosen[:, None] * points[None, :] % P_SIZE
    angle = phase.astype(jnp.float32) * (2.0 * math.pi / P_SIZE)
    factor = 1.0 / math.sqrt(P_SIZE)
    table = jnp.stack([jnp.cos(angle) * factor, -jnp.sin(angle) * factor], axis=1)
    return table.astype(jnp.bfloat16).reshape(2 * NCH, P_SIZE)


def kernel(volt_hbm, early_ref, taps_ref, table_ref, vis_ref, beam_ref,
           volt, filt, wide, send, recv, packed, pair, sums, fin, power, beams,
           load_sem, own_sem, send_sem, recv_sem, pair_send, pair_recv,
           fin_send, fin_recv, beam_send, beam_recv):
    tm, inp = lax.axis_index("tm"), lax.axis_index("inp")
    core, zlo = tm % 2, tm // 2
    zg, zq = zlo // ZQ, zlo % ZQ
    x, y, zh = inp // 8, (inp // 2) % 4, inp % 2
    width = volt.shape[1] // CHUNKS
    spectra = volt.shape[1] // P_SIZE

    loads = [
        pltpu.make_async_copy(
            volt_hbm.at[:, pl.ds(n * width, width)],
            volt.at[:, pl.ds(n * width, width)],
            load_sem.at[n],
        )
        for n in range(CHUNKS)
    ]
    for load in loads:
        load.start()

    def member(step):
        q = (zq + step // INP) % ZQ
        across = (x + (step // 2) % 4) % 4
        up = (y + (step // 8) % 4) % 4
        return q, (across * 4 + up) * 2 + (zh + step % 2) % 2

    def device(q, other):
        return ((zg * ZQ + q) * 2 + core, other)

    barrier = pltpu.get_barrier_semaphore()

    @pl.loop(1, GROUP)
    def _(step):
        pl.semaphore_signal(barrier, inc=1, device_id=device(*member(step)), device_id_type=MESH)

    for q in range(ZQ):
        pl.semaphore_signal(
            barrier, inc=1, device_id=(((1 - zg) * ZQ + q) * 2 + core, inp), device_id_type=MESH
        )
    pl.semaphore_signal(barrier, inc=1, device_id=(zlo * 2 + 1 - core, inp), device_id_type=MESH)

    coef = [jnp.broadcast_to(taps_ref[k : k + 1, :], (8, P_SIZE)) for k in range(TAPS)]
    early = early_ref[...].astype(jnp.float32)
    window = tuple(early[:, k * P_SIZE : (k + 1) * P_SIZE] for k in range(TAPS - 1))
    unroll = 8

    def filter_step(it, held):
        for u in range(unroll):
            s = it * unroll + u
            start = pl.multiple_of(s * P_SIZE, P_SIZE)
            now = volt[:, pl.ds(start, P_SIZE)].astype(jnp.float32)
            total = coef[0] * held[0]
            total = total + coef[1] * held[1]
            total = total + coef[2] * held[2]
            total = total + coef[3] * now
            row = pl.multiple_of(s * 8, 8)
            for lane in range(P_SIZE // 128):
                filt[lane, pl.ds(row, 8), :] = total[:, lane * 128 : (lane + 1) * 128]
            held = (held[1], held[2], now)
        return held

    steps = spectra // CHUNKS // unroll
    for n in range(CHUNKS):
        loads[n].wait()
        window = lax.fori_loop(n * steps, (n + 1) * steps, filter_step, window)

    table = table_ref[...]
    for i in range(8):
        block = jnp.concatenate(
            [filt[lane, pl.ds(i, spectra, stride=8), :] for lane in range(P_SIZE // 128)], axis=1
        ).astype(jnp.bfloat16)
        out = lax.dot_general(
            table, block, (((1,), (1,)), ((), ())), preferred_element_type=jnp.float32
        )
        for lane in range(spectra // 128):
            wide[lane, pl.ds(i, 2 * NCH, stride=8), :] = out[:, lane * 128 : (lane + 1) * 128]

    @pl.loop(0, 16)
    def _(it):
        rows = pl.ds(pl.multiple_of(it * 128, 128), 128)
        for lane in range(spectra // 128):
            part = wide[lane, rows, :].astype(jnp.bfloat16)
            send[pl.ds(it * 8, 8), :, :, lane * 128 : (lane + 1) * 128] = part.reshape(8, 2, 8, 128)

    mine = zq * INP + inp
    pl.semaphore_wait(barrier, GROUP - 1 + ZQ + 1)

    own = pltpu.make_async_copy(send.at[mine], recv.at[mine], own_sem)
    own.start()

    @pl.loop(1, GROUP)
    def _(step):
        q, other = member(step)
        pltpu.make_async_remote_copy(
            send.at[q * INP + other], recv.at[mine], send_sem, recv_sem,
            device_id=device(q, other), device_id_type=MESH,
        ).start()

    own.wait()
    every = recv.at[pl.ds(0, GROUP - 1)]
    pltpu.make_async_copy(every, every, recv_sem).wait()

    real = jnp.zeros((NIN, NIN), jnp.float32)
    cross = jnp.zeros((NIN, NIN), jnp.float32)
    nt = (((1,), (1,)), ((), ()))
    for z in range(ZQ):
        re = recv[z * INP : (z + 1) * INP, 0].reshape(NIN, spectra)
        im = recv[z * INP : (z + 1) * INP, 1].reshape(NIN, spectra)
        both = jnp.concatenate([re, im], axis=1)
        real += lax.dot_general(both, both, nt, preferred_element_type=jnp.float32)
        cross += lax.dot_general(im, re, nt, preferred_element_type=jnp.float32)
    row = lax.broadcasted_iota(jnp.int32, (NIN, NIN), 0)
    col = lax.broadcasted_iota(jnp.int32, (NIN, NIN), 1)
    result = jnp.where(row <= col, real, cross - cross.T) * (1.0 / (spectra * TM))
    result = result.reshape(ZLO, 2, NIN // TM, NIN)
    packed[0] = result[:, 0]
    packed[1] = result[:, 1]

    swap = pltpu.make_async_remote_copy(
        packed.at[1 - core], pair, pair_send, pair_recv,
        device_id=(zlo * 2 + 1 - core, inp), device_id_type=MESH,
    )
    swap.start()

    for z in range(ZQ):
        value = recv[z * INP : (z + 1) * INP].astype(jnp.float32)
        value = jnp.sum((value * value).reshape(INP * 2, 8, spectra), axis=0)
        power[z] = jnp.sum(value, axis=0, keepdims=True) * (1.0 / NIN)
    for step in range(1, ZQ):
        q = (zq + step) % ZQ
        pltpu.make_async_remote_copy(
            power.at[q], beams.at[zq], beam_send, beam_recv,
            device_id=device(q, inp), device_id_type=MESH,
        ).start()
    beams[zq] = power[zq]

    swap.wait()
    sums[...] = packed[core] + pair[...]
    for step in range(1, ZLO):
        z = (zlo + step) % ZLO
        pltpu.make_async_remote_copy(
            sums.at[z], fin.at[zlo], fin_send, fin_recv,
            device_id=(z * 2 + core, inp), device_id_type=MESH,
        ).start()
    fin[zlo] = sums[zlo]
    three = beams.at[pl.ds(0, ZQ - 1)]
    pltpu.make_async_copy(three, three, beam_recv).wait()
    seven = fin.at[pl.ds(0, ZLO - 1)]
    pltpu.make_async_copy(seven, seven, fin_recv).wait()
    beam_ref[...] = beams[...]
    vis_ref[...] = fin[0:ZQ] + fin[ZQ:ZLO]
    pltpu.make_async_copy(every, every, send_sem).wait()
    pltpu.make_async_copy(three, three, beam_send).wait()
    pltpu.make_async_copy(seven, seven, fin_send).wait()


def on_device(voltage, taps, chan_table):
    inputs_here, samples = voltage.shape
    spectra = samples // P_SIZE
    tail = voltage[:, (spectra - TAPS + 1) * P_SIZE :].astype(jnp.bfloat16)
    early = lax.ppermute(tail, "tm", [(i - 1, i) for i in range(1, TM)])
    table = dft_table(chan_table)
    vmem = pl.BlockSpec(memory_space=pltpu.VMEM)
    rows = NIN // TM
    f32, bf16 = jnp.float32, jnp.bfloat16
    dma = pltpu.SemaphoreType.DMA
    vis, beam = pl.pallas_call(
        kernel,
        out_shape=(
            jax.ShapeDtypeStruct((ZQ, rows, NIN), f32),
            jax.ShapeDtypeStruct((ZQ, 1, spectra), f32),
        ),
        in_specs=[pl.BlockSpec(memory_space=pl.ANY), vmem, vmem, vmem],
        out_specs=(vmem, vmem),
        scratch_shapes=[
            pltpu.VMEM((inputs_here, samples), jnp.int32),
            pltpu.VMEM((P_SIZE // 128, spectra * 8, 128), f32),
            pltpu.VMEM((spectra // 128, 2 * NCH * 8, 128), f32),
            pltpu.VMEM((GROUP, 2, 8, spectra), bf16),
            pltpu.VMEM((GROUP, 2, 8, spectra), bf16),
            pltpu.VMEM((2, ZLO, rows, NIN), f32),
            pltpu.VMEM((ZLO, rows, NIN), f32),
            pltpu.VMEM((ZLO, rows, NIN), f32),
            pltpu.VMEM((ZLO, rows, NIN), f32),
            pltpu.VMEM((ZQ, 1, spectra), f32),
            pltpu.VMEM((ZQ, 1, spectra), f32),
            dma((CHUNKS,)), dma, dma, dma, dma, dma, dma, dma, dma, dma,
        ],
        compiler_params=pltpu.CompilerParams(
            collective_id=0, has_side_effects=True, vmem_limit_bytes=40 << 20
        ),
    )(voltage, early, taps, table)
    return vis.transpose(1, 0, 2), beam.reshape(ZQ, spectra)


def solution(mesh):
    in_specs = (P("inp", "tm"), P(), P())
    out_specs = (P("tm", "inp", None), P("inp", "tm"))
    return jax.shard_map(
        on_device, mesh=mesh, in_specs=in_specs, out_specs=out_specs, check_vma=False
    )
```

time: 837 us -> 93.4 us (0.11)
  waiting for transfers between devices: 778 us -> 1.24 us
  Pallas kernels: 0 us -> 78.7 us
  starting transfers between devices: 22 us -> 4.91 us
  between operations: 15.5 us -> 0.69 us
    unnamed x4 -> x0, waiting for transfers between devices: 744 us -> none
    pallas_call x0 -> x1, Pallas kernels: none -> 78.7 us  [on_device(): pl.pallas_call(kernel, out_shape=(jax.ShapeDtypeStruct((ZQ, rows, NIN), f...]
    all_to_all x1 -> x0, waiting for transfers between devices: 31.1 us -> none  [on_device(): lax.all_to_all(spectra, 'inp', split_axis=0, concat_axis=3, tiled=True)]
    all_to_all x1 -> x0, starting transfers between devices: 17 us -> none  [on_device(): lax.all_to_all(spectra, 'inp', split_axis=0, concat_axis=3, tiled=True)]
  transfers between devices with their start and end apart: 4 -> 1, of which waited for: 4 -> 1; matrix products, arithmetic and copies ran while one was open for 1% -> 3% of each run, Pallas kernels for 0% -> 0%
where the time goes in v2:
time: 93.4 us; the launch traced here: 93.1 us
  Pallas kernels  78.7 us (84%)
  local copies, waits for them, and re-layouts  5.47 us (6%)
  starting transfers between devices  4.91 us (5%)
  other arithmetic  2.08 us (2%)
  waiting for transfers between devices  1.24 us (1%)
    pallas_call x1, Pallas kernels, on_device(): pl.pallas_call(kernel, out_shape=(jax.ShapeDtypeStruct((ZQ, rows, NIN), f...  78.7 us
    ppermute x1, starting transfers between devices, on_device(): early = lax.ppermute(tail, 'tm', [(i - 1, i) for i in range(1, TM)])  4.91 us
    unnamed x6, local copies, waits for them, and re-layouts  4.15 us
    another operation x2, other arithmetic  2.05 us
  transfers between devices with their start and end apart: 1, of which 1 were waited for; matrix products, arithmetic and copies ran while one was open for 3% of the time, Pallas kernels for 0%

profile of v2, /device:TPU:1, one launch (start us, length us, event | category | flops | bytes accessed | tf_op | source)
XLA Modules:
  0.0 93.1 jit_solution(15471684247482821498)
XLA Ops:
  0.6 0.8 slice_convert_fusion
  1.4 4.9 %collective-permute-start = (bf16[8,1536]{1,0:T(8,128)(2,1)S(1)}, bf16[8,1536]{1,0:T(8,128)(2,1)S(1)}, u32[]{:S(2)}, u32[]{:S(2)}) collective-permute-start(bf16[8,1536]{1,0:T(8,128)(2,1)S(1)} %slice_convert_fusion), channel_id=1, source_target_pairs={{0,32},{32,64},{64,96},{96,128},{128,160},{160,192},{192,224},{224... | collective-permute-start | bytes 73736 | tf_op jit(solution)/shard_map/ppermute | solution.py:193
  6.4 0.7 slice.16
  7.0 0.1 reshape.144
  7.1 0.1 copy.9
  7.2 0.1 mul.63
  7.3 1.2 %multiply_convert_fusion.1 = (bf16[128,1,512]{2,0,1:T(8,128)(2,1)S(1)}, bf16[128,1,512]{2,0,1:T(8,128)(2,1)S(1)}) fusion(s32[128]{0:T(128)S(1)} %mul.63), kind=kLoop, calls=%fused_computation.8 | loop fusion | flops 1245184 | bytes 262656 | tf_op jit(solution)/shard_map/convert
  8.6 0.3 copy.10
  8.9 0.1 convert_element_type.21.table_ref
  9.0 1.2 %collective-permute-done.early_ref = bf16[8,1536]{1,0:T(8,128)(2,1)S(1)} collective-permute-done((bf16[8,1536]{1,0:T(8,128)(2,1)S(1)}, bf16[8,1536]{1,0:T(8,128)(2,1)S(1)}, u32[]{:S(2)}, u32[]{:S(2)}) %collective-permute-start) | collective-permute-done | bytes 24608 | tf_op jit(solution)/shard_map/ppermute | solution.py:193
  10.2 0.0 copy-start
  10.2 2.2 %copy-done = s32[8,131072]{1,0:T(8,128)S(1)} copy-done((s32[8,131072]{1,0:T(8,128)S(1)}, s32[8,131072]{1,0:T(8,128)}, u32[]{:S(2)}) %copy-start) | copy-done | bytes 4194328
  12.4 0.0 copy-start.1
  12.4 0.7 copy-done.1
  13.1 78.7 %shard_map.50 = (f32[4,16,256]{2,1,0:T(8,128)S(1)}, f32[4,1,256]{2,1,0:T(1,128)S(1)}) custom-call(s32[8,131072]{1,0:T(8,128)S(1)} %copy-done, bf16[8,1536]{1,0:T(8,128)(2,1)S(1)} %collective-permute-done.early_ref, f32[4,512]{1,0:T(4,128)S(1)} %copy-done.1, bf16[256,512]{1,0:T(8,128)(2,1)S(1)} %convert_element_type.21.table_ref), custom_call_target="tpu_custom_call" | custom-call | tf_op jit(solution)/shard_map/pallas_call | solution.py:199
  91.8 0.7 copy.11
  92.5 0.6 copy.14
  (1 shorter events, 0.0 us)
Async XLA Ops:
  1.4 8.8 %collective-permute-start = (bf16[8,1536]{1,0:T(8,128)(2,1)S(1)}, bf16[8,1536]{1,0:T(8,128)(2,1)S(1)}, u32[]{:S(2)}, u32[]{:S(2)}) collective-permute-start(bf16[8,1536]{1,0:T(8,128)(2,1)S(1)} %slice_convert_fusion), channel_id=1, source_target_pairs={{0,32},{32,64},{64,96},{96,128},{128,160},{160,192},{192,224},{224... | collective-permute-start | bytes 73736 | tf_op jit(solution)/shard_map/ppermute | solution.py:193
  10.2 2.2 %copy-start = (s32[8,131072]{1,0:T(8,128)S(1)}, s32[8,131072]{1,0:T(8,128)}, u32[]{:S(2)}) copy-start(s32[8,131072]{1,0:T(8,128)} %volt_hbm.1) | copy-start | bytes 12582916
  12.4 0.7 copy-start.1

commit v3 on v2

v3 whole, which is shorter than its diff:
```python
import math

import jax
import jax.numpy as jnp
import numpy as np
from jax import lax
from jax.experimental import pallas as pl
from jax.experimental.pallas import tpu as pltpu
from jax.sharding import PartitionSpec as P

NIN = 256
P_SIZE = 512
TAPS = 4
NCH = 128
BAND = 256
ZLO, ZQ, INP = 8, 4, 32
TM = 2 * ZLO
GROUP = ZQ * INP
MESH = pl.DeviceIdType.MESH
CHUNKS = 4


def full_table():
    channel = np.arange(BAND)[:, None]
    phase = channel * np.arange(P_SIZE)[None, :] % P_SIZE
    angle = phase * (2.0 * math.pi / P_SIZE)
    factor = 1.0 / math.sqrt(P_SIZE)
    both = np.concatenate([np.cos(angle) * factor, -np.sin(angle) * factor])
    return both.astype(np.float32).astype(jnp.bfloat16)


def kernel(volt_hbm, taps_hbm, chan_hbm, full_hbm, vis_ref, beam_ref,
           volt, taps_ref, chan_ref, full_ref, tail, early, filt, wide, send, recv, packed, pair, sums, fin, power, beams,
           load_sem, taps_sem, chan_sem, full_sem, halo_send, halo_recv, own_sem, send_sem, recv_sem, pair_send, pair_recv,
           fin_send, fin_recv, beam_send, beam_recv):
    tm, inp = lax.axis_index("tm"), lax.axis_index("inp")
    core, zlo = tm % 2, tm // 2
    zg, zq = zlo // ZQ, zlo % ZQ
    x, y, zh = inp // 8, (inp // 2) % 4, inp % 2
    width = volt.shape[1] // CHUNKS
    spectra = volt.shape[1] // P_SIZE

    loads = [
        pltpu.make_async_copy(
            volt_hbm.at[:, pl.ds(n * width, width)],
            volt.at[:, pl.ds(n * width, width)],
            load_sem.at[n],
        )
        for n in range(CHUNKS)
    ]
    chan_load = pltpu.make_async_copy(chan_hbm, chan_ref, chan_sem)
    full_load = pltpu.make_async_copy(full_hbm, full_ref, full_sem)
    taps_load = pltpu.make_async_copy(taps_hbm, taps_ref, taps_sem)
    for load in [chan_load, taps_load, loads[0], full_load] + loads[1:]:
        load.start()

    def member(step):
        q = (zq + step // INP) % ZQ
        across = (x + (step // 2) % 4) % 4
        up = (y + (step // 8) % 4) % 4
        return q, (across * 4 + up) * 2 + (zh + step % 2) % 2

    def device(q, other):
        return ((zg * ZQ + q) * 2 + core, other)

    barrier = pltpu.get_barrier_semaphore()

    def greet(step):
        pl.semaphore_signal(barrier, inc=1, device_id=device(*member(step)), device_id_type=MESH)

    @pl.loop(0, GROUP // 2)
    def _(half):
        greet(2 * half + 1)

    @pl.loop(1, GROUP // 2)
    def _(half):
        greet(2 * half)

    for q in range(ZQ):
        pl.semaphore_signal(
            barrier, inc=1, device_id=(((1 - zg) * ZQ + q) * 2 + core, inp), device_id_type=MESH
        )
    pl.semaphore_signal(barrier, inc=1, device_id=(zlo * 2 + 1 - core, inp), device_id_type=MESH)

    @pl.when(jnp.logical_and(tm > 0, tm < TM - 1))
    def _():
        pl.semaphore_signal(
            barrier, inc=1, device_id=(tm + 2 * core - 1, inp), device_id_type=MESH
        )

    chan_load.wait()
    row = lax.broadcasted_iota(jnp.int32, (2 * NCH, BAND), 0)
    slot = lax.broadcasted_iota(jnp.int32, (2 * NCH, BAND), 1)
    goes = row // 2
    wanted = slot == (goes % INP) * ZQ + goes // INP
    chan = jnp.broadcast_to(chan_ref[...], (2 * NCH, BAND)).astype(jnp.float32)
    chosen = jnp.sum(jnp.where(wanted, chan, 0.0), axis=1, keepdims=True)
    lane = lax.broadcasted_iota(jnp.int32, (2 * NCH, 2 * BAND), 1)
    part = lax.broadcasted_iota(jnp.int32, (2 * NCH, 2 * BAND), 0) % 2
    pick = (lane - part * BAND).astype(jnp.float32) == chosen
    taps_load.wait()

    coef = [jnp.broadcast_to(taps_ref[k : k + 1, :], (8, P_SIZE)) for k in range(TAPS)]
    window = (jnp.zeros((8, P_SIZE), jnp.float32),) * (TAPS - 1)
    unroll = 8

    def filter_one(s, held):
        start = pl.multiple_of(s * P_SIZE, P_SIZE)
        now = volt[:, pl.ds(start, P_SIZE)].astype(jnp.float32)
        total = coef[0] * held[0]
        total = total + coef[1] * held[1]
        total = total + coef[2] * held[2]
        total = total + coef[3] * now
        row = pl.multiple_of(s * 8, 8)
        for lane in range(P_SIZE // 128):
            filt[lane, pl.ds(row, 8), :] = total[:, lane * 128 : (lane + 1) * 128]
        return (held[1], held[2], now)

    def filter_step(it, held):
        for u in range(unroll):
            held = filter_one(it * unroll + u, held)
        return held

    steps = spectra // CHUNKS // unroll
    for n in range(CHUNKS):
        loads[n].wait()
        window = lax.fori_loop(n * steps, (n + 1) * steps, filter_step, window)
    history = (TAPS - 1) * P_SIZE
    tail[...] = volt[:, pl.ds(volt.shape[1] - history, history)].astype(jnp.float32).astype(jnp.bfloat16)

    full_load.wait()
    table = jnp.dot(
        jnp.where(pick, 1.0, 0.0).astype(jnp.bfloat16), full_ref[...],
        preferred_element_type=jnp.float32,
    ).astype(jnp.bfloat16)

    def transform(tile):
        for i in range(8):
            block = jnp.concatenate(
                [
                    filt[lane, pl.ds(tile * 1024 + i, 128, stride=8), :]
                    for lane in range(P_SIZE // 128)
                ],
                axis=1,
            ).astype(jnp.bfloat16)
            wide[pl.ds(i, 2 * NCH, stride=8), :] = lax.dot_general(
                table, block, (((1,), (1,)), ((), ())), preferred_element_type=jnp.float32
            )

        @pl.loop(0, 16)
        def _(it):
            rows = pl.ds(pl.multiple_of(it * 128, 128), 128)
            ready = wide[rows, :].astype(jnp.bfloat16)
            send[pl.ds(it * 8, 8), :, :, tile * 128 : (tile + 1) * 128] = ready.reshape(8, 2, 8, 128)

    transform(1)

    mine = zq * INP + inp

    def block_power(z):
        value = recv[pl.ds(z * INP, INP)].astype(jnp.float32)
        value = jnp.sum((value * value).reshape(INP * 2, 8, spectra), axis=0)
        power[z] = jnp.sum(value, axis=0, keepdims=True) * (1.0 / NIN)

    def beam_copy(z):
        return pltpu.make_async_remote_copy(
            power.at[z], beams.at[zq], beam_send, beam_recv,
            device_id=device(z, inp), device_id_type=MESH,
        )

    ends = 1 - (tm + TM - 1) // TM + tm // (TM - 1)
    pl.semaphore_wait(barrier, GROUP - 1 + ZQ + 2 - ends)

    halo = pltpu.make_async_remote_copy(
        tail, early, halo_send, halo_recv,
        device_id=(lax.rem(tm + 1, TM), inp), device_id_type=MESH,
    )

    @pl.when(tm < TM - 1)
    def _():
        halo.start()

    def half(step, tile):
        q, other = member(step)
        lanes = pl.ds(tile * 128, 128)
        pltpu.make_async_remote_copy(
            send.at[q * INP + other, :, :, lanes], recv.at[mine, :, :, lanes],
            send_sem, recv_sem.at[0], device_id=device(q, other), device_id_type=MESH,
        ).start()

    @pl.loop(0, INP // 2)
    def _(k):
        half(2 * k + 1, 1)

    @pl.loop(1, INP // 2)
    def _(k):
        half(2 * k, 1)

    @pl.when(tm > 0)
    def _():
        halo.wait_recv()

    @pl.when(tm == 0)
    def _():
        early[...] = jnp.zeros_like(early)

    before = early[...].astype(jnp.float32)
    window = tuple(before[:, k * P_SIZE : (k + 1) * P_SIZE] for k in range(TAPS - 1))
    for s in range(TAPS - 1):
        window = filter_one(s, window)
    transform(0)
    own = pltpu.make_async_copy(send.at[mine], recv.at[mine], own_sem)
    own.start()

    @pl.loop(0, INP // 2)
    def _(k):
        half(2 * k + 1, 0)

    @pl.loop(1, INP // 2)
    def _(k):
        half(2 * k, 0)

    for ahead in range(1, ZQ):
        @pl.loop(ahead * INP, (ahead + 1) * INP)
        def _(step):
            q, other = member(step)
            pltpu.make_async_remote_copy(
                send.at[q * INP + other], recv.at[mine], send_sem, recv_sem.at[ahead],
                device_id=device(q, other), device_id_type=MESH,
            ).start()

    real = jnp.zeros((NIN, NIN), jnp.float32)
    cross = jnp.zeros((NIN, NIN), jnp.float32)
    nt = (((1,), (1,)), ((), ()))
    own.wait()
    for ahead in range(ZQ):
        z = (zq + ZQ - ahead) % ZQ
        came = recv.at[pl.ds(0, INP - (ahead == 0))]
        pltpu.make_async_copy(came, came, recv_sem.at[ahead]).wait()
        block = pl.ds(z * INP, INP)
        re = recv[block, 0].reshape(NIN, spectra)
        im = recv[block, 1].reshape(NIN, spectra)
        both = jnp.concatenate([re, im], axis=1)
        real += lax.dot_general(both, both, nt, preferred_element_type=jnp.float32)
        cross += lax.dot_general(im, re, nt, preferred_element_type=jnp.float32)
        if ahead < ZQ - 1:
            block_power(z)
            if ahead == 0:
                beams[zq] = power[zq]
            else:
                beam_copy(z).start()
    row = lax.broadcasted_iota(jnp.int32, (NIN, NIN), 0)
    col = lax.broadcasted_iota(jnp.int32, (NIN, NIN), 1)
    result = jnp.where(row <= col, real, cross - cross.T) * (1.0 / (spectra * TM))
    result = result.reshape(ZLO, 2, NIN // TM, NIN)
    packed[0] = result[:, 0]
    packed[1] = result[:, 1]

    swap = pltpu.make_async_remote_copy(
        packed.at[1 - core], pair, pair_send, pair_recv,
        device_id=(zlo * 2 + 1 - core, inp), device_id_type=MESH,
    )
    swap.start()

    last = (zq + 1) % ZQ
    block_power(last)
    beam_copy(last).start()

    swap.wait()
    sums[...] = packed[core] + pair[...]
    order = [(1 - zg) * ZQ + (zq + k) % ZQ for k in range(ZQ)]
    order += [zg * ZQ + (zq + k) % ZQ for k in range(1, ZQ)]
    for z in order:
        pltpu.make_async_remote_copy(
            sums.at[z], fin.at[zlo], fin_send, fin_recv,
            device_id=(z * 2 + core, inp), device_id_type=MESH,
        ).start()
    fin[zlo] = sums[zlo]
    three = beams.at[pl.ds(0, ZQ - 1)]
    pltpu.make_async_copy(three, three, beam_recv).wait()
    seven = fin.at[pl.ds(0, ZLO - 1)]
    pltpu.make_async_copy(seven, seven, fin_recv).wait()
    beam_ref[...] = beams[...]
    vis_ref[...] = fin[0:ZQ] + fin[ZQ:ZLO]
    every = recv.at[pl.ds(0, GROUP - 1)]
    pltpu.make_async_copy(every, every, send_sem).wait()

    @pl.when(tm < TM - 1)
    def _():
        halo.wait_send()

    pltpu.make_async_copy(three, three, beam_send).wait()
    pltpu.make_async_copy(seven, seven, fin_send).wait()


def place(vis_ref, beam_ref, vis_out, beam_out):
    for c in range(ZQ):
        vis_out[:, c, :] = vis_ref[c]
        beam_out[c : c + 1, :] = beam_ref[c]


def on_device(voltage, taps, chan_table):
    inputs_here, samples = voltage.shape
    spectra = samples // P_SIZE
    full = jnp.asarray(full_table())
    hbm = pl.BlockSpec(memory_space=pltpu.HBM)
    vmem = pl.BlockSpec(memory_space=pltpu.VMEM)
    rows = NIN // TM
    f32, bf16 = jnp.float32, jnp.bfloat16
    dma = pltpu.SemaphoreType.DMA
    vis, beam = pl.pallas_call(
        kernel,
        out_shape=(
            jax.ShapeDtypeStruct((ZQ, rows, NIN), f32),
            jax.ShapeDtypeStruct((ZQ, 1, spectra), f32),
        ),
        in_specs=[hbm, hbm, hbm, hbm],
        out_specs=(vmem, vmem),
        scratch_shapes=[
            pltpu.VMEM((inputs_here, samples), jnp.int32),
            pltpu.VMEM((TAPS, P_SIZE), f32),
            pltpu.VMEM((1, BAND), jnp.int32),
            pltpu.VMEM((2 * BAND, P_SIZE), bf16),
            pltpu.VMEM((inputs_here, (TAPS - 1) * P_SIZE), bf16),
            pltpu.VMEM((inputs_here, (TAPS - 1) * P_SIZE), bf16),
            pltpu.VMEM((P_SIZE // 128, spectra * 8, 128), f32),
            pltpu.VMEM((2 * NCH * 8, 128), f32),
            pltpu.VMEM((GROUP, 2, 8, spectra), bf16),
            pltpu.VMEM((GROUP, 2, 8, spectra), bf16),
            pltpu.VMEM((2, ZLO, rows, NIN), f32),
            pltpu.VMEM((ZLO, rows, NIN), f32),
            pltpu.VMEM((ZLO, rows, NIN), f32),
            pltpu.VMEM((ZLO, rows, NIN), f32),
            pltpu.VMEM((ZQ, 1, spectra), f32),
            pltpu.VMEM((ZQ, 1, spectra), f32),
            dma((CHUNKS,)), dma, dma, dma, dma, dma, dma, dma, dma((ZQ,)),
            dma, dma, dma, dma, dma, dma,
        ],
        compiler_params=pltpu.CompilerParams(
            collective_id=0, has_side_effects=True, vmem_limit_bytes=40 << 20
        ),
    )(*(pltpu.with_memory_space_constraint(a, pltpu.HBM) for a in (voltage, taps, chan_table.reshape(1, BAND), full)))
    return pl.pallas_call(
        place,
        out_shape=(
            jax.ShapeDtypeStruct((rows, ZQ, NIN), f32),
            jax.ShapeDtypeStruct((ZQ, spectra), f32),
        ),
        in_specs=[vmem, vmem],
        out_specs=(vmem, vmem),
        compiler_params=pltpu.CompilerParams(vmem_limit_bytes=4 << 20),
    )(vis, beam)


def solution(mesh):
    in_specs = (P("inp", "tm"), P(), P())
    out_specs = (P("tm", "inp", None), P("inp", "tm"))
    return jax.shard_map(
        on_device, mesh=mesh, in_specs=in_specs, out_specs=out_specs, check_vma=False
    )
```

time: 93.4 us -> 83.6 us (0.90); the launches traced: 93.1 us -> 82.2 us
  local copies, waits for them, and re-layouts: 5.47 us -> 0 us
  starting transfers between devices: 4.91 us -> 0 us
  Pallas kernels: 78.7 us -> 81.6 us
  other arithmetic: 2.08 us -> 0 us
  waiting for transfers between devices: 1.24 us -> 0 us
    ppermute x1 -> x0, starting transfers between devices: 4.91 us -> none  [on_device(): early = lax.ppermute(tail, 'tm', [(i - 1, i) for i in range(1, TM)])]
    unnamed x6 -> x0, local copies, waits for them, and re-layouts: 4.15 us -> none
    pallas_call x1, Pallas kernels: 78.7 us -> 80.9 us  [on_device(): pl.pallas_call(kernel, out_shape=(jax.ShapeDtypeStruct((ZQ, rows, NIN), f...]
    another operation x3 -> x0, other arithmetic: 2.08 us -> none
    ppermute x1 -> x0, waiting for transfers between devices: 1.24 us -> none  [on_device(): early = lax.ppermute(tail, 'tm', [(i - 1, i) for i in range(1, TM)])]
  transfers between devices with their start and end apart: 1 -> 0, of which waited for: 1 -> 0; matrix products, arithmetic and copies ran while one was open for 3% -> 0% of each run, Pallas kernels for 0% -> 0%
where the time goes in v3:
time: 83.6 us; the launch traced here: 82.2 us
  Pallas kernels  81.6 us (98%)
    pallas_call x1, Pallas kernels, on_device(): pl.pallas_call(kernel, out_shape=(jax.ShapeDtypeStruct((ZQ, rows, NIN), f...  80.9 us

profile of v3, /device:TPU:1, one launch (start us, length us, event | category | flops | bytes accessed | tf_op | source)
XLA Modules:
  0.0 82.2 jit_solution(2373867660704418105)
XLA Ops:
  0.6 80.9 %shard_map.59 = (f32[4,16,256]{2,1,0:T(8,128)S(1)}, f32[4,1,256]{2,1,0:T(1,128)S(1)}) custom-call(s32[8,131072]{1,0:T(8,128)} %volt_hbm.1, f32[4,512]{1,0:T(4,128)} %taps_hbm.1, s32[1,256]{1,0:T(1,128)} %bitcast.1, bf16[512,512]{1,0:T(8,128)(2,1)} %constant.2.clone.full_hbm), custom_call_target="tpu_custom_call" | custom-call | tf_op jit(solution)/shard_map/pallas_call | solution.py:311
  81.5 0.7 shard_map.60

commit v4 on v3

--- a/solution.py
+++ b/solution.py
@@ -18,6 +18,7 @@
 GROUP = ZQ * INP
 MESH = pl.DeviceIdType.MESH
 CHUNKS = 4
+PHASES = (0, 1, 3, 2)
 
 
 def full_table():
@@ -54,27 +55,33 @@
     for load in [chan_load, taps_load, loads[0], full_load] + loads[1:]:
         load.start()
 
-    def member(step):
-        q = (zq + step // INP) % ZQ
+    def chip(phase):
+        return (zq // 2 + phase // 2) % 2 * 2 + (zq + phase) % 2
+
+    def member(phase, step):
         across = (x + (step // 2) % 4) % 4
         up = (y + (step // 8) % 4) % 4
-        return q, (across * 4 + up) * 2 + (zh + step % 2) % 2
+        return chip(phase), (across * 4 + up) * 2 + (zh + step % 2) % 2
 
     def device(q, other):
         return ((zg * ZQ + q) * 2 + core, other)
 
     barrier = pltpu.get_barrier_semaphore()
 
-    def greet(step):
-        pl.semaphore_signal(barrier, inc=1, device_id=device(*member(step)), device_id_type=MESH)
-
-    @pl.loop(0, GROUP // 2)
-    def _(half):
-        greet(2 * half + 1)
-
-    @pl.loop(1, GROUP // 2)
-    def _(half):
-        greet(2 * half)
+    def greet(phase, step):
+        pl.semaphore_signal(
+            barrier, inc=1, device_id=device(*member(phase, step)), device_id_type=MESH
+        )
+
+    for phase in PHASES:
+        @pl.loop(0, INP // 2)
+        def _(k):
+            greet(phase, 2 * k + 1)
+
+    for phase in PHASES:
+        @pl.loop(int(phase == 0), INP // 2)
+        def _(k):
+            greet(phase, 2 * k)
 
     for q in range(ZQ):
         pl.semaphore_signal(
@@ -181,7 +188,7 @@
         halo.start()
 
     def half(step, tile):
-        q, other = member(step)
+        q, other = member(0, step)
         lanes = pl.ds(tile * 128, 128)
         pltpu.make_async_remote_copy(
             send.at[q * INP + other, :, :, lanes], recv.at[mine, :, :, lanes],
@@ -220,32 +227,40 @@
     def _(k):
         half(2 * k, 0)
 
-    for ahead in range(1, ZQ):
-        @pl.loop(ahead * INP, (ahead + 1) * INP)
+    def whole(phase, step):
+        q, other = member(phase, step)
+        pltpu.make_async_remote_copy(
+            send.at[q * INP + other], recv.at[mine], send_sem, recv_sem.at[phase],
+            device_id=device(q, other), device_id_type=MESH,
+        ).start()
+
+    for phase in PHASES[1:-1]:
+        @pl.loop(0, INP)
         def _(step):
-            q, other = member(step)
-            pltpu.make_async_remote_copy(
-                send.at[q * INP + other], recv.at[mine], send_sem, recv_sem.at[ahead],
-                device_id=device(q, other), device_id_type=MESH,
-            ).start()
+            whole(phase, step)
+
+    for far in (1, 0):
+        @pl.loop(0, INP // 2)
+        def _(k):
+            whole(PHASES[-1], 2 * k + far)
 
     real = jnp.zeros((NIN, NIN), jnp.float32)
     cross = jnp.zeros((NIN, NIN), jnp.float32)
     nt = (((1,), (1,)), ((), ()))
     own.wait()
-    for ahead in range(ZQ):
-        z = (zq + ZQ - ahead) % ZQ
-        came = recv.at[pl.ds(0, INP - (ahead == 0))]
-        pltpu.make_async_copy(came, came, recv_sem.at[ahead]).wait()
+    for phase in PHASES:
+        z = chip(phase)
+        came = recv.at[pl.ds(0, INP - (phase == 0))]
+        pltpu.make_async_copy(came, came, recv_sem.at[phase]).wait()
         block = pl.ds(z * INP, INP)
         re = recv[block, 0].reshape(NIN, spectra)
         im = recv[block, 1].reshape(NIN, spectra)
         both = jnp.concatenate([re, im], axis=1)
         real += lax.dot_general(both, both, nt, preferred_element_type=jnp.float32)
         cross += lax.dot_general(im, re, nt, preferred_element_type=jnp.float32)
-        if ahead < ZQ - 1:
+        if phase != PHASES[-1]:
             block_power(z)
-            if ahead == 0:
+            if phase == 0:
                 beams[zq] = power[zq]
             else:
                 beam_copy(z).start()
@@ -256,25 +271,32 @@
     packed[0] = result[:, 0]
     packed[1] = result[:, 1]
 
-    swap = pltpu.make_async_remote_copy(
-        packed.at[1 - core], pair, pair_send, pair_recv,
-        device_id=(zlo * 2 + 1 - core, inp), device_id_type=MESH,
-    )
-    swap.start()
-
-    last = (zq + 1) % ZQ
+    halves = [pl.ds((1 - zg) * ZQ, ZQ), pl.ds(zg * ZQ, ZQ)]
+    swaps = [
+        pltpu.make_async_remote_copy(
+            packed.at[1 - core, rows], pair.at[rows], pair_send.at[n], pair_recv.at[n],
+            device_id=(zlo * 2 + 1 - core, inp), device_id_type=MESH,
+        )
+        for n, rows in enumerate(halves)
+    ]
+    for swap in swaps:
+        swap.start()
+
+    last = chip(PHASES[-1])
     block_power(last)
     beam_copy(last).start()
 
-    swap.wait()
-    sums[...] = packed[core] + pair[...]
-    order = [(1 - zg) * ZQ + (zq + k) % ZQ for k in range(ZQ)]
-    order += [zg * ZQ + (zq + k) % ZQ for k in range(1, ZQ)]
-    for z in order:
+    def rows_to(z):
         pltpu.make_async_remote_copy(
             sums.at[z], fin.at[zlo], fin_send, fin_recv,
             device_id=(z * 2 + core, inp), device_id_type=MESH,
         ).start()
+
+    for n, rows in enumerate(halves):
+        swaps[n].wait()
+        sums[rows] = packed[core, rows] + pair[rows]
+        for k in range(n, ZQ):
+            rows_to((zg + 1 - n) % 2 * ZQ + (zq + k) % ZQ)
     fin[zlo] = sums[zlo]
     three = beams.at[pl.ds(0, ZQ - 1)]
     pltpu.make_async_copy(three, three, beam_recv).wait()
@@ -334,7 +356,7 @@
             pltpu.VMEM((ZQ, 1, spectra), f32),
             pltpu.VMEM((ZQ, 1, spectra), f32),
             dma((CHUNKS,)), dma, dma, dma, dma, dma, dma, dma, dma((ZQ,)),
-            dma, dma, dma, dma, dma, dma,
+            dma((2,)), dma((2,)), dma, dma, dma, dma,
         ],
         compiler_params=pltpu.CompilerParams(
             collective_id=0, has_side_effects=True, vmem_limit_bytes=40 << 20

time: 83.6 us -> 83.1 us (level); the launches traced: 82.2 us -> 83 us
  no operation moved by 1% of the time
where the time goes in v4:
time: 83.1 us; the launch traced here: 83 us
  Pallas kernels  82.4 us (99%)
    pallas_call x1, Pallas kernels, on_device(): pl.pallas_call(kernel, out_shape=(jax.ShapeDtypeStruct((ZQ, rows, NIN), f...  81.7 us

profile of v4, /device:TPU:1, one launch (start us, length us, event | category | flops | bytes accessed | tf_op | source)
XLA Modules:
  0.0 83.0 jit_solution(6900484098887490804)
XLA Ops:
  0.6 81.7 %shard_map.59 = (f32[4,16,256]{2,1,0:T(8,128)S(1)}, f32[4,1,256]{2,1,0:T(1,128)S(1)}) custom-call(s32[8,131072]{1,0:T(8,128)} %volt_hbm.1, f32[4,512]{1,0:T(4,128)} %taps_hbm.1, s32[1,256]{1,0:T(1,128)} %bitcast.1, bf16[512,512]{1,0:T(8,128)(2,1)} %constant.2.clone.full_hbm), custom_call_target="tpu_custom_call" | custom-call | tf_op jit(solution)/shard_map/pallas_call | solution.py:333
  82.3 0.7 shard_map.60
